TPU v7x, 32 devices: a whole 2x2x4 slice. The times are simulated.
32 devices in a mesh: ctx: 8 (over z, x), fsdp: 4 (over y, core).
Axes of the slice: x: 2, y: 2, z: 4, core: 2. Of those that a mesh axis runs over, the one named last changes fastest.
Arguments:
- layer_input: bfloat16 [2, 4, 1024, 1024], P(None, 'fsdp', 'ctx'), may hold values from -6 to 6
- segments: int32 [2, 4, 1024], P(None, 'fsdp', 'ctx'), may hold values from 0 to 15, never falling along the last dimension, each value on 1 to 512 neighbouring positions
- cotangent: bfloat16 [2, 4, 1024, 1024], P(None, 'fsdp', 'ctx'), may hold values from -6 to 6
- query_weight: bfloat16 [1024, 1024], P('fsdp'), may hold values from -0.1875 to 0.1875
- key_weight: bfloat16 [1024, 1024], P('fsdp'), may hold values from -0.1875 to 0.1875
- value_weight: bfloat16 [1024, 1024], P('fsdp'), may hold values from -0.1875 to 0.1875
- output_weight: bfloat16 [1024, 1024], P('fsdp'), may hold values from -0.75 to 0.75
- expand_weight: bfloat16 [1024, 4096], P('fsdp'), may hold values from -0.1875 to 0.1875
- contract_weight: bfloat16 [4096, 1024], P('fsdp'), may hold values from -0.09375 to 0.09375
- query_bias: bfloat16 [1024], P('fsdp'), may hold values from -3 to 3
- value_bias: bfloat16 [1024], P('fsdp'), may hold values from -3 to 3
- output_bias: bfloat16 [1024], P('fsdp'), may hold values from -3 to 3
- first_gain: bfloat16 [1024], P('fsdp'), may hold values from 0.099609375 to 1.8984375
- first_shift: bfloat16 [1024], P('fsdp'), may hold values from -3 to 3
- expand_bias: bfloat16 [4096], P('fsdp'), may hold values from -3 to 3
- contract_bias: bfloat16 [1024], P('fsdp'), may hold values from -3 to 3
- second_gain: bfloat16 [1024], P('fsdp'), may hold values from 0.099609375 to 1.8984375
- second_shift: bfloat16 [1024], P('fsdp'), may hold values from -3 to 3
Outputs:
- layer_output: bfloat16 [2, 4, 1024, 1024], P(None, 'fsdp', 'ctx')
- input_grad: float32 [2, 4, 1024, 1024], P(None, 'fsdp', 'ctx')
- query_weight_grad: float32 [1024, 1024], P('fsdp')
- key_weight_grad: float32 [1024, 1024], P('fsdp')
- value_weight_grad: float32 [1024, 1024], P('fsdp')
- output_weight_grad: float32 [1024, 1024], P('fsdp')
- expand_weight_grad: float32 [1024, 4096], P('fsdp')
- contract_weight_grad: float32 [4096, 1024], P('fsdp')
- query_bias_grad: float32 [1024], P('fsdp')
- value_bias_grad: float32 [1024], P('fsdp')
- output_bias_grad: float32 [1024], P('fsdp')
- first_gain_grad: float32 [1024], P('fsdp')
- first_shift_grad: float32 [1024], P('fsdp')
- expand_bias_grad: float32 [4096], P('fsdp')
- contract_bias_grad: float32 [1024], P('fsdp')
- second_gain_grad: float32 [1024], P('fsdp')
- second_shift_grad: float32 [1024], P('fsdp')
Inputs may be any that keep to these rules, and one draw needn't show every extreme that they name: `segments`: in each sequence the ids never fall along the positions; each document holds 1 to 512 positions, and one holds exactly 512.
All inputs are finite; a program needn't handle non-finite values.
Results may differ from a plain program's by a relative error of at most 0.025.
Values may be sent and summed in bfloat16 or wider, within the bound.
A program may use at most 192 MiB of HBM per device.

v0:
```python
import jax
import jax.numpy as jnp
from jax import lax
from jax.sharding import PartitionSpec as P

HEADS = 16
HEAD_DIM = 64


def as_sent(x):
    return jax.tree.map(lambda a: a.astype(jnp.bfloat16) if a.dtype == jnp.float32 else a, x)


def plain_dot(left_side, right_side):
    return jnp.dot(left_side, right_side, preferred_element_type=jnp.float32)


def left_dot(left_side, right_side):
    return lax.dot_general(
        left_side, right_side, (((0,), (0,)), ((), ())), preferred_element_type=jnp.float32
    )


def right_dot(left_side, right_side):
    return lax.dot_general(
        left_side, right_side, (((1,), (1,)), ((), ())), preferred_element_type=jnp.float32
    )


def norm_forward(hidden, gain_row, offset_row):
    centre = hidden - jnp.mean(hidden, axis=-1, keepdims=True)
    inverse = lax.rsqrt(jnp.mean(centre * centre, axis=-1, keepdims=True) + 1e-05)
    normed = centre * inverse
    return (normed * gain_row.astype(jnp.float32) + offset_row.astype(jnp.float32), normed, inverse)


def norm_backward(grad_out, normed, inverse, gain_row):
    scaled = grad_out * gain_row.astype(jnp.float32)
    grad_in = inverse * (
        scaled
        - jnp.mean(scaled, axis=-1, keepdims=True)
        - normed * jnp.mean(scaled * normed, axis=-1, keepdims=True)
    )
    return (grad_in, jnp.sum(grad_out * normed, axis=0), jnp.sum(grad_out, axis=0))


def gather_weights(shards):
    return (
        lax.all_gather(shards[0], "fsdp", axis=0, tiled=True),
        lax.all_gather(shards[1], "fsdp", axis=0, tiled=True),
        lax.all_gather(shards[2], "fsdp", axis=0, tiled=True),
        lax.all_gather(shards[3], "fsdp", axis=0, tiled=True),
        lax.all_gather(shards[4], "fsdp", axis=0, tiled=True),
        lax.all_gather(shards[5], "fsdp", axis=0, tiled=True),
        lax.all_gather(shards[6], "fsdp", axis=0, tiled=True),
        lax.all_gather(shards[7], "fsdp", axis=0, tiled=True),
        lax.all_gather(shards[8], "fsdp", axis=0, tiled=True),
        lax.all_gather(shards[9], "fsdp", axis=0, tiled=True),
        lax.all_gather(shards[10], "fsdp", axis=0, tiled=True),
        lax.all_gather(shards[11], "fsdp", axis=0, tiled=True),
        lax.all_gather(shards[12], "fsdp", axis=0, tiled=True),
        lax.all_gather(shards[13], "fsdp", axis=0, tiled=True),
        lax.all_gather(shards[14], "fsdp", axis=0, tiled=True),
    )


def attend_forward(query_bf, key_bf, value_bf, seg_local):
    row_count = query_bf.shape[0]
    score_scale = HEAD_DIM ** (-0.5)
    query_heads = query_bf.reshape(row_count, HEADS, HEAD_DIM)
    run_max = jnp.full((HEADS, row_count), -1e30, jnp.float32)
    key_rows = lax.all_gather(key_bf, "ctx", axis=0, tiled=True)
    value_rows = lax.all_gather(value_bf, "ctx", axis=0, tiled=True)
    key_seg = lax.all_gather(seg_local, "ctx", axis=0, tiled=True)
    piece_rows = key_rows.shape[0]
    key_heads = key_rows.reshape(piece_rows, HEADS, HEAD_DIM)
    value_heads = value_rows.reshape(piece_rows, HEADS, HEAD_DIM)
    scores = (
        jnp.einsum("rhd,khd->hrk", query_heads, key_heads, preferred_element_type=jnp.float32)
        * score_scale
    )
    same_doc = seg_local[:, None] == key_seg[None, :]
    scores = jnp.where(same_doc[None], scores, -1e30)
    new_max = jnp.maximum(run_max, jnp.max(scores, axis=-1))
    numerators = jnp.exp(scores - new_max[..., None])
    run_sum = jnp.sum(numerators, axis=-1)
    accumulated = jnp.einsum(
        "hrk,khd->hrd",
        numerators.astype(jnp.bfloat16),
        value_heads,
        preferred_element_type=jnp.float32,
    )
    run_max, run_sum, accumulated = (new_max, run_sum, accumulated)
    context = jnp.transpose(accumulated / run_sum[..., None], (1, 0, 2)).reshape(
        row_count, HEADS * HEAD_DIM
    )
    return (context, run_max + jnp.log(run_sum))


def block_grads(
    query_heads, grad_heads, query_seg, log_sum, row_delta, key_heads, value_heads, key_seg
):
    score_scale = HEAD_DIM ** (-0.5)
    scores = (
        jnp.einsum("rhd,khd->hrk", query_heads, key_heads, preferred_element_type=jnp.float32)
        * score_scale
    )
    same_doc = query_seg[:, None] == key_seg[None, :]
    scores = jnp.where(same_doc[None], scores, -1e30)
    probs_full = jnp.exp(scores - log_sum[..., None])
    grad_probs = jnp.einsum(
        "rhd,khd->hrk", grad_heads, value_heads, preferred_element_type=jnp.float32
    )
    grad_scores = (probs_full * (grad_probs - row_delta[..., None])).astype(jnp.bfloat16)
    return (probs_full, grad_scores)


def attend_backward(query_bf, key_bf, value_bf, seg_local, context, log_sum, grad_context):
    row_count = query_bf.shape[0]
    score_scale = HEAD_DIM ** (-0.5)
    key_every, value_every, seg_every = (
        lax.all_gather(key_bf, "ctx", axis=0, tiled=True),
        lax.all_gather(value_bf, "ctx", axis=0, tiled=True),
        lax.all_gather(seg_local, "ctx", axis=0, tiled=True),
    )
    length = key_every.shape[0]
    block_len = min(512, length)
    query_heads = query_bf.reshape(row_count, HEADS, HEAD_DIM)
    grad_heads = grad_context.reshape(row_count, HEADS, HEAD_DIM)
    row_delta = jnp.sum(
        (grad_context.astype(jnp.float32) * context).reshape(row_count, HEADS, HEAD_DIM), axis=-1
    ).T

    def visit_block(grad_query, block_num):
        first_row = block_num * block_len
        key_heads = lax.dynamic_slice_in_dim(key_every, first_row, block_len, 0).reshape(
            block_len, HEADS, HEAD_DIM
        )
        value_heads = lax.dynamic_slice_in_dim(value_every, first_row, block_len, 0).reshape(
            block_len, HEADS, HEAD_DIM
        )
        key_seg = lax.dynamic_slice_in_dim(seg_every, first_row, block_len, 0)
        probs_full, grad_scores = block_grads(
            query_heads, grad_heads, seg_local, log_sum, row_delta, key_heads, value_heads, key_seg
        )
        grad_query = (
            grad_query
            + jnp.einsum("hrk,khd->rhd", grad_scores, key_heads, preferred_element_type=jnp.float32)
            * score_scale
        )
        grad_keys = (
            jnp.einsum("hrk,rhd->khd", grad_scores, query_heads, preferred_element_type=jnp.float32)
            * score_scale
        )
        grad_values = jnp.einsum(
            "hrk,rhd->khd",
            probs_full.astype(jnp.bfloat16),
            grad_heads,
            preferred_element_type=jnp.float32,
        )
        stacked = jnp.stack(
            (
                grad_keys.reshape(block_len, HEADS * HEAD_DIM),
                grad_values.reshape(block_len, HEADS * HEAD_DIM),
            ),
            axis=1,
        )
        return (grad_query, stacked)

    grad_query, pieces = lax.scan(
        visit_block,
        jnp.zeros((row_count, HEADS, HEAD_DIM), jnp.float32),
        jnp.arange(length // block_len),
    )
    key_terms = pieces.reshape(length, 2, HEADS * HEAD_DIM)
    own_rows = lax.psum_scatter(
        key_terms.astype(jnp.bfloat16), "ctx", scatter_dimension=0, tiled=True
    ).astype(jnp.float32)
    grad_keyed = own_rows[:, 0].astype(jnp.bfloat16)
    grad_valued = own_rows[:, 1].astype(jnp.bfloat16)
    grad_queries = grad_query.reshape(row_count, HEADS * HEAD_DIM).astype(jnp.bfloat16)
    return (grad_queries, grad_keyed, grad_valued)


def layer_forward(inputs, seg_local, full_weights):
    (
        query_weight,
        key_weight,
        value_weight,
        output_weight,
        expand_weight,
        contract_weight,
        query_bias,
        value_bias,
        output_bias,
        first_gain,
        first_shift,
        expand_bias,
        contract_bias,
        second_gain,
        second_shift,
    ) = full_weights
    query_bf = (plain_dot(inputs, query_weight) + query_bias.astype(jnp.float32)).astype(
        jnp.bfloat16
    )
    key_bf = plain_dot(inputs, key_weight).astype(jnp.bfloat16)
    value_bf = (plain_dot(inputs, value_weight) + value_bias.astype(jnp.float32)).astype(
        jnp.bfloat16
    )
    context, log_sum = attend_forward(query_bf, key_bf, value_bf, seg_local)
    context_bf = context.astype(jnp.bfloat16)
    first_sum = (
        inputs.astype(jnp.float32)
        + plain_dot(context_bf, output_weight)
        + output_bias.astype(jnp.float32)
    )
    first_out, normed_one, inverse_one = norm_forward(first_sum, first_gain, first_shift)
    first_bf = first_out.astype(jnp.bfloat16)
    hidden = plain_dot(first_bf, expand_weight) + expand_bias.astype(jnp.float32)
    gelled_bf = jax.nn.gelu(hidden, approximate=False).astype(jnp.bfloat16)
    second_sum = (
        first_out + plain_dot(gelled_bf, contract_weight) + contract_bias.astype(jnp.float32)
    )
    result, normed_two, inverse_two = norm_forward(second_sum, second_gain, second_shift)
    kept_state = (
        query_bf,
        key_bf,
        value_bf,
        context,
        log_sum,
        context_bf,
        normed_one,
        inverse_one,
        first_bf,
        hidden,
        gelled_bf,
        normed_two,
        inverse_two,
    )
    return (result.astype(jnp.bfloat16), kept_state)


def layer_backward(inputs, seg_local, grad_out, kept_state, full_weights):
    (
        query_weight,
        key_weight,
        value_weight,
        output_weight,
        expand_weight,
        contract_weight,
        query_bias,
        value_bias,
        output_bias,
        first_gain,
        first_shift,
        expand_bias,
        contract_bias,
        second_gain,
        second_shift,
    ) = full_weights
    (
        query_bf,
        key_bf,
        value_bf,
        context,
        log_sum,
        context_bf,
        normed_one,
        inverse_one,
        first_bf,
        hidden,
        gelled_bf,
        normed_two,
        inverse_two,
    ) = kept_state
    grad_second, second_gain_grad, second_shift_grad = norm_backward(
        grad_out.astype(jnp.float32), normed_two, inverse_two, second_gain
    )
    grad_branch = grad_second.astype(jnp.bfloat16)
    contract_weight_grad = left_dot(gelled_bf, grad_branch)
    contract_bias_grad = jnp.sum(grad_branch.astype(jnp.float32), axis=0)
    grad_gelled = right_dot(grad_branch, contract_weight)
    gelu_pull = jax.vjp(lambda values: jax.nn.gelu(values, approximate=False), hidden)[1]
    grad_hidden = gelu_pull(grad_gelled)[0].astype(jnp.bfloat16)
    expand_weight_grad = left_dot(first_bf, grad_hidden)
    expand_bias_grad = jnp.sum(grad_hidden.astype(jnp.float32), axis=0)
    grad_first = grad_second + right_dot(grad_hidden, expand_weight)
    grad_attn, first_gain_grad, first_shift_grad = norm_backward(
        grad_first, normed_one, inverse_one, first_gain
    )
    grad_attn_low = grad_attn.astype(jnp.bfloat16)
    output_weight_grad = left_dot(context_bf, grad_attn_low)
    output_bias_grad = jnp.sum(grad_attn_low.astype(jnp.float32), axis=0)
    grad_context = right_dot(grad_attn_low, output_weight).astype(jnp.bfloat16)
    grad_queries, grad_keyed, grad_valued = attend_backward(
        query_bf, key_bf, value_bf, seg_local, context, log_sum, grad_context
    )
    query_weight_grad = left_dot(inputs, grad_queries)
    key_weight_grad = left_dot(inputs, grad_keyed)
    value_weight_grad = left_dot(inputs, grad_valued)
    query_bias_grad = jnp.sum(grad_queries.astype(jnp.float32), axis=0)
    value_bias_grad = jnp.sum(grad_valued.astype(jnp.float32), axis=0)
    grad_input = (
        grad_attn
        + right_dot(grad_queries, query_weight)
        + right_dot(grad_keyed, key_weight)
        + right_dot(grad_valued, value_weight)
    )
    grad_terms = (
        query_weight_grad,
        key_weight_grad,
        value_weight_grad,
        output_weight_grad,
        expand_weight_grad,
        contract_weight_grad,
        query_bias_grad,
        value_bias_grad,
        output_bias_grad,
        first_gain_grad,
        first_shift_grad,
        expand_bias_grad,
        contract_bias_grad,
        second_gain_grad,
        second_shift_grad,
    )
    return (grad_input, grad_terms)


def per_device(
    layer_input,
    segments,
    cotangent,
    query_weight,
    key_weight,
    value_weight,
    output_weight,
    expand_weight,
    contract_weight,
    query_bias,
    value_bias,
    output_bias,
    first_gain,
    first_shift,
    expand_bias,
    contract_bias,
    second_gain,
    second_shift,
):
    shards = (
        query_weight,
        key_weight,
        value_weight,
        output_weight,
        expand_weight,
        contract_weight,
        query_bias,
        value_bias,
        output_bias,
        first_gain,
        first_shift,
        expand_bias,
        contract_bias,
        second_gain,
        second_shift,
    )
    micro_count = layer_input.shape[0]
    results = []
    grad_inputs = []
    totals = None
    for micro_step in range(micro_count):
        inputs = layer_input[micro_step, 0]
        seg_local = segments[micro_step, 0].astype(jnp.bfloat16)
        front_weights = gather_weights(shards)
        result, kept_state = layer_forward(inputs, seg_local, front_weights)
        behind = gather_weights(shards)
        grad_input, grad_terms = layer_backward(
            inputs, seg_local, cotangent[micro_step, 0], kept_state, behind
        )
        results.append(result)
        grad_inputs.append(grad_input)
        if totals is None:
            totals = grad_terms
        else:
            totals = tuple(
                (left_side + right_side for left_side, right_side in zip(totals, grad_terms))
            )
    reduced = jax.tree.map(
        lambda part: part.astype(jnp.float32),
        lax.psum_scatter(as_sent(totals), "fsdp", scatter_dimension=0, tiled=True),
    )
    summed = jax.tree.map(lambda part: part.astype(jnp.float32), lax.psum(as_sent(reduced), "ctx"))
    layer_output = jnp.stack(results, axis=0)[:, None]
    input_grad = jnp.stack(grad_inputs, axis=0)[:, None]
    return (
        layer_output,
        input_grad,
        summed[0],
        summed[1],
        summed[2],
        summed[3],
        summed[4],
        summed[5],
        summed[6],
        summed[7],
        summed[8],
        summed[9],
        summed[10],
        summed[11],
        summed[12],
        summed[13],
        summed[14],
    )


def solution(mesh):
    in_specs = (
        P(None, "fsdp", "ctx", None),
        P(None, "fsdp", "ctx"),
        P(None, "fsdp", "ctx", None),
        P("fsdp", None),
        P("fsdp", None),
        P("fsdp", None),
        P("fsdp", None),
        P("fsdp", None),
        P("fsdp", None),
        P("fsdp"),
        P("fsdp"),
        P("fsdp"),
        P("fsdp"),
        P("fsdp"),
        P("fsdp"),
        P("fsdp"),
        P("fsdp"),
        P("fsdp"),
    )
    out_specs = (
        P(None, "fsdp", "ctx", None),
        P(None, "fsdp", "ctx", None),
        P("fsdp", None),
        P("fsdp", None),
        P("fsdp", None),
        P("fsdp", None),
        P("fsdp", None),
        P("fsdp", None),
        P("fsdp"),
        P("fsdp"),
        P("fsdp"),
        P("fsdp"),
        P("fsdp"),
        P("fsdp"),
        P("fsdp"),
        P("fsdp"),
        P("fsdp"),
    )
    return jax.shard_map(
        per_device, mesh=mesh, in_specs=in_specs, out_specs=out_specs, check_vma=False
    )
```

profile of v0, /device:TPU:0, one launch (start us, length us, event | category | flops | bytes accessed | tf_op | source)
XLA Modules:
  0.0 1220.2 jit_solution(14195021096110765214)
XLA Ops:
  10.1 6.0 all-gather.3
  16.1 18.8 %all-gather.27.cloned.1.call-done = bf16[1024,1024]{1,0:T(8,128)(2,1)} async-done(((bf16[256,1024]{1,0:T(8,128)(2,1)}), bf16[1024,1024]{1,0:T(8,128)(2,1)}) %all-gather.27.cloned.1.call-update) | async-done | bytes 2097168 | tf_op jit(solution)/shard_map/all_gather | solution.py:51
  34.9 2.8 fusion.68
  37.8 21.3 %all-gather.23.cloned.1.call-done = bf16[1024,1024]{1,0:T(8,128)(2,1)} async-done(((bf16[256,1024]{1,0:T(8,128)(2,1)}), bf16[1024,1024]{1,0:T(8,128)(2,1)}) %all-gather.23.cloned.1.call-update) | async-done | bytes 2097168 | tf_op jit(solution)/shard_map/all_gather | solution.py:50
  59.1 2.7 convolution_convert_fusion.3
  63.1 2.7 convolution_convert_fusion.2
  68.2 5.1 all-gather.7
  73.3 5.2 all_gather.55
  78.4 5.1 all-gather.4
  83.5 5.1 all-gather.2
  88.6 5.1 all-gather.6
  93.7 5.1 all-gather.5
  98.8 5.1 all-gather.8
  103.9 20.6 %all-gather = bf16[1,1,1024]{2,1,0:T(2,128)(2,1)S(1)} all-gather(bf16[1,1,128]{2,1,0:T(2,128)(2,1)S(1)} %get-tuple-element.466), channel_id=2, replica_groups=mesh['ctx'=8,'fsdp'=4] {'ctx'}, dimensions={2}, use_global_device_ids=true | all-gather | bytes 2304 | tf_op jit(solution)/shard_map/all_gather | solution.py:74
  124.6 16.3 %all-gather.1 = bf16[1,1,1024]{2,1,0:T(2,128)(2,1)S(1)} all-gather(bf16[1,1,128]{2,1,0:T(2,128)(2,1)S(1)} %get-tuple-element.465), channel_id=3, replica_groups=mesh['ctx'=8,'fsdp'=4] {'ctx'}, dimensions={2}, use_global_device_ids=true | all-gather | bytes 2304 | tf_op jit(solution)/shard_map/all_gather | solution.py:74
  140.9 5.4 all-gather.9
  150.3 4.0 copy.99
  154.3 31.3 %all-gather.25.cloned.1.call-done = bf16[1024,1024]{1,0:T(8,128)(2,1)} async-done(((bf16[128,1024]{1,0:T(8,128)(2,1)}), bf16[1024,1024]{1,0:T(8,128)(2,1)}) %all-gather.25.cloned.1.call-update) | async-done | bytes 2097168 | tf_op jit(solution)/shard_map/all_gather | solution.py:72
  185.6 3.9 copy.98
  189.6 3.2 fusion.28
  194.9 3.6 fusion.74
  199.6 36.4 %all-gather.39.cloned.1.call-done = bf16[1024,1024]{1,0:T(8,128)(2,1)} async-done(((bf16[128,1024]{1,0:T(8,128)(2,1)}), bf16[1024,1024]{1,0:T(8,128)(2,1)}) %all-gather.39.cloned.1.call-update) | async-done | bytes 2097168 | tf_op jit(solution)/shard_map/all_gather | solution.py:73
  236.0 3.9 copy.102
  239.9 46.6 %all-gather.37.cloned.1.call-done = bf16[1024,1024]{1,0:T(8,128)(2,1)} async-done(((bf16[128,1024]{1,0:T(8,128)(2,1)}), bf16[1024,1024]{1,0:T(8,128)(2,1)}) %all-gather.37.cloned.1.call-update) | async-done | bytes 2097168 | tf_op jit(solution)/shard_map/all_gather | solution.py:72
  286.5 3.9 copy.101
  290.4 18.7 %all-gather.31.cloned.1.call-done = bf16[1024,1024]{1,0:T(8,128)(2,1)} async-done(((bf16[256,1024]{1,0:T(8,128)(2,1)}), bf16[1024,1024]{1,0:T(8,128)(2,1)}) %all-gather.31.cloned.1.call-update) | async-done | bytes 2097168 | tf_op jit(solution)/shard_map/all_gather | solution.py:52
  311.6 3.2 fusion.29
  317.0 4.4 fusion.71
  323.0 46.0 %all-gather.33.cloned.1.call-done = bf16[1024,4096]{1,0:T(8,128)(2,1)} async-done(((bf16[256,4096]{1,0:T(8,128)(2,1)}), bf16[1024,4096]{1,0:T(8,128)(2,1)}) %all-gather.33.cloned.1.call-update) | async-done | bytes 8388624 | tf_op jit(solution)/shard_map/all_gather | solution.py:53
  369.1 6.1 convolution_add_fusion.1
  375.2 53.7 %all-gather.35.cloned.1.call-done = bf16[4096,1024]{1,0:T(8,128)(2,1)} async-done(((bf16[1024,1024]{1,0:T(8,128)(2,1)}), bf16[4096,1024]{1,0:T(8,128)(2,1)}) %all-gather.35.cloned.1.call-update) | async-done | bytes 8388624 | tf_op jit(solution)/shard_map/all_gather | solution.py:54
  428.9 9.7 fusion.170
  442.2 5.7 fusion.172
  451.1 8.1 convert_reduce_fusion.1
  459.2 3.7 multiply_reduce_fusion.1
  462.9 8.1 convert_reduce_fusion
  471.0 4.4 convert_reduce_fusion.7
  477.3 2.5 broadcast.394.clone2.1
  479.9 34.4 %while.26 = (s32[]{:T(128)}, f32[128,16,64]{0,2,1:T(8,128)}, bf16[2,512,2,1024]{3,1,0,2:T(8,128)(2,1)}, s32[2]{0:T(128)S(1)}, bf16[1024,1024]{0,1:T(8,128)(2,1)}...) while((s32[]{:T(128)}, f32[128,16,64]{0,2,1:T(8,128)}, ...), condition=%wide.region_18.19_spmd.clone, body=%wide.region_17.18_spmd.clone.sunk | while | flops 684130304 | bytes 77819448 | solution.py:170
  492.5 3.0 copy.170
  509.8 3.0 copy.170
  520.9 2.5 broadcast.394.clone2
  523.5 34.9 %while.27 = (s32[]{:T(128)}, f32[128,16,64]{0,2,1:T(8,128)}, bf16[2,512,2,1024]{3,1,0,2:T(8,128)(2,1)}, s32[2]{0:T(128)S(1)}, bf16[1024,1024]{0,1:T(8,128)(2,1)}...) while((s32[]{:T(128)}, f32[128,16,64]{0,2,1:T(8,128)}, ...), condition=%wide.region_26.27_spmd.clone, body=%wide.region_25.26_spmd.clone.sunk | while | flops 684130304 | bytes 77819448 | solution.py:170
  536.5 3.0 copy.171
  546.8 2.5 fusion.285
  553.8 3.0 copy.171
  566.6 35.8 %reduce-scatter.9.cloned.1.call-done = bf16[128,2,1024]{2,0,1:T(8,128)(2,1)} async-done(((bf16[1024,2,1024]{2,0,1:T(8,128)(2,1)}), bf16[128,2,1024]{2,0,1:T(8,128)(2,1)}) %reduce-scatter.9.cloned.1.call-update) | async-done | bytes 524304 | tf_op jit(solution)/shard_map/reduce_scatter | solution.py:176
  602.4 3.7 fusion.111
  606.1 88.5 %reduce-scatter.11.cloned.1.call-done = bf16[128,2,1024]{2,0,1:T(8,128)(2,1)} async-done(((bf16[1024,2,1024]{2,0,1:T(8,128)(2,1)}), bf16[128,2,1024]{2,0,1:T(8,128)(2,1)}) %reduce-scatter.11.cloned.1.call-update) | async-done | bytes 524304 | tf_op jit(solution)/shard_map/reduce_scatter | solution.py:176
  694.7 4.3 fusion.53
  704.2 8.2 fusion.164
  712.5 11.8 add_convert_fusion.1
  725.9 10.9 fusion.148
  736.8 12.7 %add_convert_fusion = bf16[4096,1024]{1,0:T(8,128)(2,1)} fusion(f32[4096,1024]{1,0:T(8,128)} %fusion.148, f32[128,1024]{1,0:T(8,128)S(1)} %copy-done.51, f32[128,4096]{1,0:T(8,128)S(1)} %copy-done.46), kind=kOutput, calls=%fused_computation.44 | convolution fusion | flops 1116340224 | bytes 27787264 | tf_op jit(solution)/shard_map/dot_general | solution.py:19
  749.9 12.6 %reduce-scatter.19.cloned.1.call-done = bf16[256,1024]{1,0:T(8,128)(2,1)} async-done(((bf16[1024,1024]{1,0:T(8,128)(2,1)}), bf16[256,1024]{1,0:T(8,128)(2,1)}) %reduce-scatter.19.cloned.1.call-update) | async-done | bytes 524304 | tf_op jit(solution)/shard_map/reduce_scatter | solution.py:389
  762.4 34.4 %reduce-scatter.15.cloned.1.call-done = bf16[256,1024]{0,1:T(8,128)(2,1)} async-done(((bf16[1024,1024]{0,1:T(8,128)(2,1)}), bf16[256,1024]{0,1:T(8,128)(2,1)}) %reduce-scatter.15.cloned.1.call-update) | async-done | bytes 524304 | tf_op jit(solution)/shard_map/reduce_scatter | solution.py:389
  796.8 34.6 %reduce-scatter.17.cloned.1.call-done = bf16[256,1024]{0,1:T(8,128)(2,1)} async-done(((bf16[1024,1024]{0,1:T(8,128)(2,1)}), bf16[256,1024]{0,1:T(8,128)(2,1)}) %reduce-scatter.17.cloned.1.call-update) | async-done | bytes 524304 | tf_op jit(solution)/shard_map/reduce_scatter | solution.py:389
  831.4 74.2 %reduce-scatter.21.cloned.1.call-done = bf16[256,4096]{1,0:T(8,128)(2,1)} async-done(((bf16[1024,4096]{1,0:T(8,128)(2,1)}), bf16[256,4096]{1,0:T(8,128)(2,1)}) %reduce-scatter.21.cloned.1.call-update) | async-done | bytes 2097168 | tf_op jit(solution)/shard_map/reduce_scatter | solution.py:389
  905.6 74.4 %reduce-scatter.23.cloned.1.call-done = bf16[1024,1024]{1,0:T(8,128)(2,1)} async-done(((bf16[4096,1024]{1,0:T(8,128)(2,1)}), bf16[1024,1024]{1,0:T(8,128)(2,1)}) %reduce-scatter.23.cloned.1.call-update) | async-done | bytes 2097168 | tf_op jit(solution)/shard_map/reduce_scatter | solution.py:389
  985.7 2.6 convolution_add_fusion.4
  990.1 11.3 all-reduce.11
  1002.0 23.1 %all-reduce.9 = (bf16[256]{0:T(256)(128)(2,1)S(1)}, bf16[256]{0:T(256)(128)(2,1)S(1)}, bf16[256]{0:T(256)(128)(2,1)S(1)}, bf16[256]{0:T(256)(128)(2,1)S(1)}, bf1...) all-reduce(bf16[256]{0:T(256)(128)(2,1)S(1)} %dynamic-slice.1, ...), channel_id=1, replica_groups=mesh['ctx'=8,'fsdp'=4] {'ctx'}, use_global_device_ids=true, to_apply=%region_43.44 | all-reduce | flops 3072 | bytes 12288 | tf_op jit(solution)/shard_map/psum | solution.py:391
  1030.3 2.6 convolution_add_fusion.3
  1037.3 164.2 %all-reduce.14.cloned.1.call-done = (bf16[256,1024]{0,1:T(8,128)(2,1)}, bf16[256,1024]{0,1:T(8,128)(2,1)}, bf16[256,1024]{0,1:T(8,128)(2,1)}, bf16[256,1024]{1,0...) async-done(((bf16[256,1024]{0,1:T(8,128)(2,1)}, bf16[256,1024]{0,1:T(8,128)(2,1)}, bf16[256,1024]{0,1:T(8,128)(2,1)}, bf16[256,1024]{1,0:T(8,128)(2,1)}, ...) | async-done | bytes 6291472 | tf_op jit(solution)/shard_map/psum | solution.py:391
  (424 shorter events, 129.6 us)
Async XLA Ops:
  7.2 27.7 %all-gather.27.cloned.1.call-start = ((), (), s32[]{:S(2)}) async-start(), calls=%async_computation.11 | async-start | bytes 2621440 | tf_op jit(solution)/shard_map/all_gather | solution.py:51
  7.9 51.2 %copy-start.13 = (bf16[2,1,128,1024]{3,2,1,0:T(8,128)(2,1)S(1)}, bf16[2,1,128,1024]{3,2,1,0:T(8,128)(2,1)}, u32[]{:S(2)}) copy-start(bf16[2,1,128,1024]{3,2,1,0:T(8,128)(2,1)} %param.22) | copy-start | bytes 1572868
  7.9 51.2 %all-gather.23.cloned.1.call-start = ((), (), s32[]{:S(2)}) async-start(), calls=%async_computation.9 | async-start | bytes 2621440 | tf_op jit(solution)/shard_map/all_gather | solution.py:50
  8.7 138.5 %all-gather.21.cloned.1.call-start = ((), (), s32[]{:S(2)}) async-start(), calls=%async_computation.8 | async-start | bytes 2621440 | tf_op jit(solution)/shard_map/all_gather | solution.py:49
  9.4 140.9 %all-gather.29.cloned.1.call-start = ((), (), s32[]{:S(2)}) async-start(), calls=%async_computation.12 | async-start | bytes 2359296 | tf_op jit(solution)/shard_map/all_gather | solution.py:73
  37.7 24.2 %copy-start.6 = (bf16[1024,1024]{1,0:T(8,128)(2,1)S(1)}, bf16[1024,1024]{1,0:T(8,128)(2,1)}, u32[]{:S(2)}) copy-start(bf16[1024,1024]{1,0:T(8,128)(2,1)} %all-gather.27.cloned.1.call-done) | copy-start | bytes 6291460
  37.8 147.9 %all-gather.25.cloned.1.call-start = ((), (), s32[]{:S(2)}) async-start(), calls=%async_computation.10 | async-start | bytes 2359296 | tf_op jit(solution)/shard_map/all_gather | solution.py:72
  61.9 174.1 %all-gather.39.cloned.1.call-start = ((), (), s32[]{:S(2)}) async-start(), calls=%async_computation.17 | async-start | bytes 2359296 | tf_op jit(solution)/shard_map/all_gather | solution.py:73
  63.1 223.4 %all-gather.37.cloned.1.call-start = ((), (), s32[]{:S(2)}) async-start(), calls=%async_computation.16 | async-start | bytes 2359296 | tf_op jit(solution)/shard_map/all_gather | solution.py:72
  65.9 243.3 %all-gather.31.cloned.1.call-start = ((), (), s32[]{:S(2)}) async-start(), calls=%async_computation.13 | async-start | bytes 2621440 | tf_op jit(solution)/shard_map/all_gather | solution.py:52
  66.7 6.6 copy-start.89
  66.7 11.7 copy-start.93
  66.7 16.8 %copy-start.90 = (s32[2,1,128]{2,1,0:T(1,128)S(1)}, s32[2,1,128]{2,1,0:T(1,128)}, u32[]{:S(2)}) copy-start(s32[2,1,128]{2,1,0:T(1,128)} %param.23) | copy-start | bytes 3076
  66.7 16.8 %copy-start.94 = (bf16[256]{0:T(256)(128)(2,1)S(1)}, bf16[256]{0:T(256)(128)(2,1)}, u32[]{:S(2)}) copy-start(bf16[256]{0:T(256)(128)(2,1)} %param.31) | copy-start | bytes 1540
  66.7 21.9 %copy-start.95 = (bf16[256]{0:T(256)(128)(2,1)S(1)}, bf16[256]{0:T(256)(128)(2,1)}, u32[]{:S(2)}) copy-start(bf16[256]{0:T(256)(128)(2,1)} %param.35) | copy-start | bytes 1540
  66.7 27.0 %copy-start.96 = (bf16[256]{0:T(256)(128)(2,1)S(1)}, bf16[256]{0:T(256)(128)(2,1)}, u32[]{:S(2)}) copy-start(bf16[256]{0:T(256)(128)(2,1)} %param.34) | copy-start | bytes 1540
  66.8 32.1 %copy-start.97 = (bf16[256]{0:T(256)(128)(2,1)S(1)}, bf16[256]{0:T(256)(128)(2,1)}, u32[]{:S(2)}) copy-start(bf16[256]{0:T(256)(128)(2,1)} %param.38) | copy-start | bytes 1540
  66.8 74.1 %copy-start.98 = (bf16[256]{0:T(256)(128)(2,1)S(1)}, bf16[256]{0:T(256)(128)(2,1)}, u32[]{:S(2)}) copy-start(bf16[256]{0:T(256)(128)(2,1)} %param.39) | copy-start | bytes 1540
  66.8 302.3 %all-gather.33.cloned.1.call-start = ((), (), s32[]{:S(2)}) async-start(), calls=%async_computation.14 | async-start | bytes 10485760 | tf_op jit(solution)/shard_map/all_gather | solution.py:53
  67.5 361.4 %all-gather.35.cloned.1.call-start = ((), (), s32[]{:S(2)}) async-start(), calls=%async_computation.15 | async-start | bytes 10485760 | tf_op jit(solution)/shard_map/all_gather | solution.py:54
  68.1 534.3 %reduce-scatter.9.cloned.1.call-start = ((), (), s32[]{:S(2)}) async-start(), calls=%async_computation.18 | async-start | bytes 4718592 | tf_op jit(solution)/shard_map/reduce_scatter | solution.py:176
  93.7 346.5 %copy-start.56 = (f32[4,1,256]{2,1,0:T(1,128)}, f32[4,1,256]{2,1,0:T(1,128)S(1)}, u32[]{:S(2)}) copy-start(f32[4,1,256]{2,1,0:T(1,128)S(1)} %convert_element_type.499) | copy-start | bytes 12292
  103.9 46.1 %copy-start.70 = (bf16[128]{0:T(256)(128)(2,1)}, bf16[128]{0:T(256)(128)(2,1)S(1)}, u32[]{:S(2)}) copy-start(bf16[128]{0:T(256)(128)(2,1)S(1)} %get-tuple-element.654) | copy-start | bytes 772
  103.9 46.1 %copy-start.72 = (bf16[128]{0:T(256)(128)(2,1)}, bf16[128]{0:T(256)(128)(2,1)S(1)}, u32[]{:S(2)}) copy-start(bf16[128]{0:T(256)(128)(2,1)S(1)} %get-tuple-element.702) | copy-start | bytes 772
  124.6 25.5 %copy-start.66 = (bf16[1024]{0:T(1024)(128)(2,1)}, bf16[1024]{0:T(1024)(128)(2,1)S(1)}, u32[]{:S(2)}) copy-start(bf16[1024]{0:T(1024)(128)(2,1)S(1)} %reduce.4) | copy-start | bytes 6148
  140.9 9.2 copy-start.64
  150.2 161.3 %copy-start.4 = (bf16[128,1024]{0,1:T(8,128)(2,1)}, bf16[128,1024]{0,1:T(8,128)(2,1)S(1)}, u32[]{:S(2)}) copy-start(bf16[128,1024]{0,1:T(8,128)(2,1)S(1)} %copy.100) | copy-start | bytes 786436
  198.6 110.6 %copy-start.31 = (f32[128,16,64]{0,2,1:T(8,128)}, f32[128,16,64]{0,2,1:T(8,128)S(1)}, u32[]{:S(2)}) copy-start(f32[128,16,64]{0,2,1:T(8,128)S(1)} %fusion.74) | copy-start | bytes 1572868
  290.4 21.1 %copy-start.54 = (pred[128,1024]{1,0:T(8,128)(4,1)S(1)}, pred[128,1024]{1,0:T(8,128)(4,1)}, u32[]{:S(2)}) copy-start(pred[128,1024]{1,0:T(8,128)(4,1)} %broadcast_compare_fusion.2) | copy-start | bytes 393220
  311.3 159.6 %copy-start.15 = (f32[128,1024]{1,0:T(8,128)}, f32[128,1024]{1,0:T(8,128)S(1)}, u32[]{:S(2)}) copy-start(f32[128,1024]{1,0:T(8,128)S(1)} %get-tuple-element.470) | copy-start | bytes 1572868
  311.3 159.6 %copy-start.74 = (f32[128]{0:T(128)}, f32[128]{0:T(128)S(1)}, u32[]{:S(2)}) copy-start(f32[128]{0:T(128)S(1)} %broadcast_multiply_fusion.11) | copy-start | bytes 1540
  323.0 148.0 %copy-start.76 = (f32[128]{0:T(128)}, f32[128]{0:T(128)S(1)}, u32[]{:S(2)}) copy-start(f32[128]{0:T(128)S(1)} %add_rsqrt_fusion.3) | copy-start | bytes 1540
  428.9 9.9 slice-start
  428.9 9.9 slice-start.1
  428.9 9.9 copy-start.18
  442.2 20.6 %copy-start.45 = (f32[128,4096]{1,0:T(8,128)}, f32[128,4096]{1,0:T(8,128)S(1)}, u32[]{:S(2)}) copy-start(f32[128,4096]{1,0:T(8,128)S(1)} %convolution_add_fusion) | copy-start | bytes 6291460
  442.2 5.9 copy-start.30
  451.1 8.1 copy-start.52
  451.1 19.9 %copy-start.50 = (f32[128,1024]{1,0:T(8,128)}, f32[128,1024]{1,0:T(8,128)S(1)}, u32[]{:S(2)}) copy-start(f32[128,1024]{1,0:T(8,128)S(1)} %get-tuple-element.439) | copy-start | bytes 1572868
  514.4 180.3 %reduce-scatter.11.cloned.1.call-start = ((), (), s32[]{:S(2)}) async-start(), calls=%async_computation.19 | async-start | bytes 4718592 | tf_op jit(solution)/shard_map/reduce_scatter | solution.py:176
  558.4 191.5 %reduce-scatter.13.cloned.1.call-start = ((), (), s32[]{:S(2)}) async-start(), calls=%async_computation.20 | async-start | bytes 2621440 | tf_op jit(solution)/shard_map/reduce_scatter | solution.py:389
  562.7 199.7 %reduce-scatter.19.cloned.1.call-start = ((), (), s32[]{:S(2)}) async-start(), calls=%async_computation.23 | async-start | bytes 2621440 | tf_op jit(solution)/shard_map/reduce_scatter | solution.py:389
  566.6 230.2 %reduce-scatter.15.cloned.1.call-start = ((), (), s32[]{:S(2)}) async-start(), calls=%async_computation.21 | async-start | bytes 2621440 | tf_op jit(solution)/shard_map/reduce_scatter | solution.py:389
  699.0 132.4 %reduce-scatter.17.cloned.1.call-start = ((), (), s32[]{:S(2)}) async-start(), calls=%async_computation.22 | async-start | bytes 2621440 | tf_op jit(solution)/shard_map/reduce_scatter | solution.py:389
  702.9 9.6 copy-start.20
  702.9 202.7 %reduce-scatter.21.cloned.1.call-start = ((), (), s32[]{:S(2)}) async-start(), calls=%async_computation.24 | async-start | bytes 10485760 | tf_op jit(solution)/shard_map/reduce_scatter | solution.py:389
  704.2 8.2 copy-start.36
  724.3 255.6 %reduce-scatter.23.cloned.1.call-start = ((), (), s32[]{:S(2)}) async-start(), calls=%async_computation.25 | async-start | bytes 10485760 | tf_op jit(solution)/shard_map/reduce_scatter | solution.py:389
  725.9 10.9 copy-start.46
  725.9 10.9 copy-start.51
  749.6 451.9 %all-reduce.14.cloned.1.call-start = ((), (), s32[]{:S(2)}) async-start(), calls=%async_computation.26 | async-start | bytes 12582912 | tf_op jit(solution)/shard_map/psum | solution.py:391
  979.9 5.6 copy-start.85
  979.9 5.7 copy-start.78
  980.0 5.7 copy-start.84
  980.0 5.7 copy-start.82
  980.0 5.7 copy-start.83
  980.0 5.7 copy-start.80
  980.0 5.7 copy-start.81
  980.0 5.7 copy-start.87
  980.0 5.7 copy-start.88
  980.0 5.7 copy-start.10
  990.0 42.9 %copy-start.7 = (bf16[1024,1024]{1,0:T(8,128)(2,1)S(1)}, bf16[1024,1024]{1,0:T(8,128)(2,1)}, u32[]{:S(2)}) copy-start(bf16[1024,1024]{1,0:T(8,128)(2,1)} %all-gather.27.cloned.1.call-done) | copy-start | bytes 6291460
  990.0 42.9 %copy-start.41 = (bf16[128,2,1024]{2,0,1:T(8,128)(2,1)S(1)}, bf16[128,2,1024]{2,0,1:T(8,128)(2,1)}, u32[]{:S(2)}) copy-start(bf16[128,2,1024]{2,0,1:T(8,128)(2,1)} %reduce-scatter.11.cloned.1.call-done) | copy-start | bytes 1572868
  1201.5 5.9 copy-start.58
  (63 other events, 138.7 us)
Sparse Core Ops, SparseCore 0:
  9.6 25.2 all-gather.26
  36.5 22.5 all-gather.22
  60.7 22.6 all-gather.20
  85.9 49.3 all-gather.28
  137.8 47.7 all-gather.24
  188.2 47.7 all-gather.38
  238.7 47.7 all-gather.36
  288.1 21.0 all-gather.30
  310.8 58.2 all-gather.32
  370.5 58.3 all-gather.34
  514.5 87.8 reduce-scatter.8
  606.9 87.6 reduce-scatter.10
  697.2 31.1 reduce-scatter.12
  730.9 31.4 reduce-scatter.18
  765.4 31.4 reduce-scatter.14
  799.9 31.3 reduce-scatter.16
  833.8 71.7 reduce-scatter.20
  908.2 71.6 reduce-scatter.22
  984.9 216.5 all-reduce.13
where the time goes:
time: 1230 us; the launch traced here: 1220 us
  waiting for transfers between devices  796 us (65%)
  matrix products  178 us (14%)
  blocking collectives  118 us (10%)
  local copies, waits for them, and re-layouts  74.1 us (6%)
  other arithmetic  32.8 us (3%)
  between operations  16.8 us (1%)
    reduce_scatter x6, waiting for transfers between devices, per_device(): lax.psum_scatter(as_sent(totals), 'fsdp', scatter_dimension=0, tiled=True)  230 us
    psum x1, waiting for transfers between devices, per_device(): lax.psum(as_sent(reduced), 'ctx')  164 us
    reduce_scatter x2, waiting for transfers between devices, attend_backward(): lax.psum_scatter(key_terms.astype(jnp.bfloat16), 'ctx', scatter_dimension...  124 us
    all_gather x2, waiting for transfers between devices, attend_forward(): key_rows = lax.all_gather(key_bf, 'ctx', axis=0, tiled=True)  77.9 us
    dot_general x12, matrix products, left_dot(): lax.dot_general(left_side, right_side, (((0,), (0,)), ((), ())), preferre...  60 us
    all_gather x1, waiting for transfers between devices, gather_weights(): lax.all_gather(shards[5], 'fsdp', axis=0, tiled=True)  53.7 us
    all_gather x1, waiting for transfers between devices, gather_weights(): lax.all_gather(shards[4], 'fsdp', axis=0, tiled=True)  46 us
    dot_general x12, matrix products, plain_dot(): return jnp.dot(left_side, right_side, preferred_element_type=jnp.float32)  37.6 us
  transfers between devices with their start and end apart: 19, of which 16 were waited for; matrix products, arithmetic and copies ran while one was open for 15% of the time, Pallas kernels for 0%

commit v1 on v0

--- a/solution.py
+++ b/solution.py
@@ -1,3 +1,4 @@
+import functools
 import jax
 import jax.numpy as jnp
 from jax import lax
@@ -5,6 +6,26 @@
 
 HEADS = 16
 HEAD_DIM = 64
+
+
+def _extend_grid(state, chip_axis):
+    taken_in, piece_out, arr_next = (
+        jax.lax.psum(1, chip_axis),
+        jax.lax.axis_index(chip_axis),
+        state.shape[0],
+    )
+    outer, reached = (state, 1)
+    while reached < taken_in:
+        all_blocks = []
+        for num in tuple(range(taken_in)):
+            all_blocks.append((num, (num - reached) % taken_in))
+        outer = jnp.concatenate([outer, jax.lax.ppermute(outer, chip_axis, all_blocks)], axis=0)
+        reached = 2 * reached
+    z2 = jnp.roll(outer, piece_out * arr_next, axis=0)
+    return z2
+
+
+wait_the_stops_all = functools.partial(_extend_grid, chip_axis="fsdp")
 
 
 def as_sent(x):
@@ -51,7 +72,7 @@
         lax.all_gather(shards[2], "fsdp", axis=0, tiled=True),
         lax.all_gather(shards[3], "fsdp", axis=0, tiled=True),
         lax.all_gather(shards[4], "fsdp", axis=0, tiled=True),
-        lax.all_gather(shards[5], "fsdp", axis=0, tiled=True),
+        wait_the_stops_all(shards[5]),
         lax.all_gather(shards[6], "fsdp", axis=0, tiled=True),
         lax.all_gather(shards[7], "fsdp", axis=0, tiled=True),
         lax.all_gather(shards[8], "fsdp", axis=0, tiled=True),

time: 1230 us -> 1180 us (0.959)
  waiting for transfers between devices: 796 us -> 638 us
  blocking collectives: 118 us -> 205 us
  other arithmetic: 32.8 us -> 53.9 us
    all_gather x1, blocking collectives: 5.08 us -> 92.5 us  [gather_weights(): lax.all_gather(shards[12], 'fsdp', axis=0, tiled=True)]
    all_gather x2, waiting for transfers between devices: 77.9 us -> 0.01 us  [attend_forward(): key_rows = lax.all_gather(key_bf, 'ctx', axis=0, tiled=True)]
    all_gather x1 -> x0, waiting for transfers between devices: 53.7 us -> none  [gather_weights(): lax.all_gather(shards[5], 'fsdp', axis=0, tiled=True)]
    all_gather x2, waiting for transfers between devices: 36.4 us -> 0.01 us  [attend_forward(): value_rows = lax.all_gather(value_bf, 'ctx', axis=0, tiled=True)]
    ppermute x0 -> x2, waiting for transfers between devices: none -> 34.2 us  [_extend_grid(): jax.lax.ppermute(outer, chip_axis, all_blocks)]
    concatenate x0 -> x2, other arithmetic: none -> 21.1 us  [the longest x1 17 us: _extend_grid(): z2 = jnp.roll(outer, piece_out * arr_next, axis=0)]
    all_gather x1, waiting for transfers between devices: 18.7 us -> 0.01 us  [gather_weights(): lax.all_gather(shards[3], 'fsdp', axis=0, tiled=True)]
  transfers between devices with their start and end apart: 19 -> 20, of which waited for: 16 -> 12; matrix products, arithmetic and copies ran while one was open for 15% -> 17% of each run, Pallas kernels for 0% -> 0%
where the time goes in v1:
time: 1180 us; the launch traced here: 1170 us
  waiting for transfers between devices  638 us (54%)
  blocking collectives  205 us (17%)
  matrix products  177 us (15%)
  local copies, waits for them, and re-layouts  72.1 us (6%)
  other arithmetic  53.9 us (5%)
  between operations  17.3 us (1%)
    reduce_scatter x6, waiting for transfers between devices, per_device(): lax.psum_scatter(as_sent(totals), 'fsdp', scatter_dimension=0, tiled=True)  230 us
    psum x1, waiting for transfers between devices, per_device(): lax.psum(as_sent(reduced), 'ctx')  164 us
    reduce_scatter x2, waiting for transfers between devices, attend_backward(): lax.psum_scatter(key_terms.astype(jnp.bfloat16), 'ctx', scatter_dimension...  125 us
    all_gather x1, blocking collectives, gather_weights(): lax.all_gather(shards[12], 'fsdp', axis=0, tiled=True)  92.5 us
    dot_general x12, matrix products, left_dot(): lax.dot_general(left_side, right_side, (((0,), (0,)), ((), ())), preferre...  60 us
    all_gather x1, waiting for transfers between devices, gather_weights(): lax.all_gather(shards[4], 'fsdp', axis=0, tiled=True)  41.1 us
    all_gather x2, blocking collectives, attend_forward(): key_seg = lax.all_gather(seg_local, 'ctx', axis=0, tiled=True)  36.6 us
    dot_general x12, matrix products, right_dot(): lax.dot_general(left_side, right_side, (((1,), (1,)), ((), ())), preferre...  36.4 us
  transfers between devices with their start and end apart: 20, of which 12 were waited for; matrix products, arithmetic and copies ran while one was open for 17% of the time, Pallas kernels for 0%

profile of v1, /device:TPU:0, one launch (start us, length us, event | category | flops | bytes accessed | tf_op | source)
XLA Modules:
  0.0 1169.8 jit_solution(15967095938438934123)
XLA Ops:
  10.1 6.0 all-gather.3
  16.1 18.8 %all-gather.26.cloned.1.call-done = bf16[1024,1024]{1,0:T(8,128)(2,1)} async-done(((bf16[256,1024]{1,0:T(8,128)(2,1)}), bf16[1024,1024]{1,0:T(8,128)(2,1)}) %all-gather.26.cloned.1.call-update) | async-done | bytes 2097168 | tf_op jit(solution)/shard_map/all_gather | solution.py:72
  34.9 2.8 fusion.73
  37.8 21.3 %all-gather.22.cloned.1.call-done = bf16[1024,1024]{1,0:T(8,128)(2,1)} async-done(((bf16[256,1024]{1,0:T(8,128)(2,1)}), bf16[1024,1024]{1,0:T(8,128)(2,1)}) %all-gather.22.cloned.1.call-update) | async-done | bytes 2097168 | tf_op jit(solution)/shard_map/all_gather | solution.py:71
  59.1 2.7 convolution_convert_fusion.3
  63.1 2.9 convolution_convert_fusion.2
  67.7 34.2 %collective-permute-done = bf16[1024,1024]{1,0:T(8,128)(2,1)} collective-permute-done((bf16[1024,1024]{1,0:T(8,128)(2,1)S(1)}, bf16[1024,1024]{1,0:T(8,128)(2,1)}, u32[]{:S(2)}, u32[]{:S(2)}) %collective-permute-start) | collective-permute-done | bytes 2097184 | tf_op jit(solution)/shard_map/ppermute | solution.py:22
  101.9 4.0 pad_maximum_fusion
  107.6 92.5 %all-gather.7 = bf16[4,1,256]{2,1,0:T(2,128)(2,1)S(1)} all-gather(bf16[1,1,256]{2,1,0:T(2,128)(2,1)S(1)} %reshape.371), channel_id=1, replica_groups=mesh['ctx'=8,'fsdp'=4] {'fsdp'}, dimensions={0}, use_global_device_ids=true | all-gather | bytes 2560 | tf_op jit(solution)/shard_map/all_gather | solution.py:82
  200.1 5.5 all_gather.53
  205.6 5.1 all-gather.4
  210.7 5.1 all-gather.2
  215.8 5.1 all-gather.6
  220.9 5.1 all-gather.5
  226.0 5.1 all-gather.8
  231.1 20.4 %all-gather = bf16[1,1,1024]{2,1,0:T(2,128)(2,1)S(1)} all-gather(bf16[1,1,128]{2,1,0:T(2,128)(2,1)S(1)} %get-tuple-element.467), channel_id=2, replica_groups=mesh['ctx'=8,'fsdp'=4] {'ctx'}, dimensions={2}, use_global_device_ids=true | all-gather | bytes 2304 | tf_op jit(solution)/shard_map/all_gather | solution.py:95
  251.5 16.2 %all-gather.1 = bf16[1,1,1024]{2,1,0:T(2,128)(2,1)S(1)} all-gather(bf16[1,1,128]{2,1,0:T(2,128)(2,1)S(1)} %get-tuple-element.466), channel_id=3, replica_groups=mesh['ctx'=8,'fsdp'=4] {'ctx'}, dimensions={2}, use_global_device_ids=true | all-gather | bytes 2304 | tf_op jit(solution)/shard_map/all_gather | solution.py:95
  267.7 5.1 all-gather.9
  276.9 17.0 %fusion.30 = bf16[4096,1024]{1,0:T(8,128)(2,1)} fusion(s32[]{:T(128)S(6)} %select_n.41, bf16[1024,1024]{1,0:T(8,128)(2,1)} %param.32, bf16[1024,1024]{1,0:T(8,128)(2,1)} %collective-permute-done, bf16[2048,1024]{1,0:T(8,128)(2,1)} %collective-permute-done.1), kind=kLoop, calls=%fused_computation.54 | loop fusion | flops 50331648 | bytes 16777220 | tf_op jit(solution)/shard_map/jit(_roll_dynamic)/concatenate | solution.py:24
  293.9 3.9 copy.99
  297.8 4.0 copy.98
  301.8 3.2 fusion.33
  307.2 3.6 fusion.79
  311.8 4.0 copy.102
  315.8 3.9 copy.101
  322.2 3.5 fusion.34
  327.8 4.0 fusion.76
  333.5 41.1 %all-gather.32.cloned.1.call-done = bf16[1024,4096]{1,0:T(8,128)(2,1)} async-done(((bf16[256,4096]{1,0:T(8,128)(2,1)}), bf16[1024,4096]{1,0:T(8,128)(2,1)}) %all-gather.32.cloned.1.call-update) | async-done | bytes 8388624 | tf_op jit(solution)/shard_map/all_gather | solution.py:74
  374.6 4.9 convolution_add_fusion.1
  379.6 9.5 fusion.175
  390.7 5.5 fusion.177
  399.4 8.1 convert_reduce_fusion.1
  407.5 3.7 multiply_reduce_fusion.1
  411.2 8.1 convert_reduce_fusion
  419.3 4.4 convert_reduce_fusion.7
  425.6 2.5 broadcast.395.clone2.1
  428.2 34.8 %while.26 = (s32[]{:T(128)}, f32[128,16,64]{0,2,1:T(8,128)}, bf16[2,512,2,1024]{3,1,0,2:T(8,128)(2,1)}, s32[2]{0:T(128)S(1)}, bf16[1024,1024]{0,1:T(8,128)(2,1)}...) while((s32[]{:T(128)}, f32[128,16,64]{0,2,1:T(8,128)}, ...), condition=%wide.region_18.20_spmd.clone, body=%wide.region_17.19_spmd.clone.sunk | while | flops 684130304 | bytes 77819448 | solution.py:191
  441.2 3.0 copy.170
  451.5 2.5 fusion.276
  458.5 3.0 copy.170
  469.6 2.5 broadcast.395.clone2
  472.1 34.7 %while.27 = (s32[]{:T(128)}, f32[128,16,64]{0,2,1:T(8,128)}, bf16[2,512,2,1024]{3,1,0,2:T(8,128)(2,1)}, s32[2]{0:T(128)S(1)}, bf16[1024,1024]{0,1:T(8,128)(2,1)}...) while((s32[]{:T(128)}, f32[128,16,64]{0,2,1:T(8,128)}, ...), condition=%wide.region_26.28_spmd.clone, body=%wide.region_25.27_spmd.clone.sunk | while | flops 684130304 | bytes 77819448 | solution.py:191
  485.0 3.0 copy.171
  495.3 2.5 fusion.290
  502.4 3.0 copy.171
  515.2 36.1 %reduce-scatter.9.cloned.1.call-done = bf16[128,2,1024]{2,0,1:T(8,128)(2,1)} async-done(((bf16[1024,2,1024]{2,0,1:T(8,128)(2,1)}), bf16[128,2,1024]{2,0,1:T(8,128)(2,1)}) %reduce-scatter.9.cloned.1.call-update) | async-done | bytes 524304 | tf_op jit(solution)/shard_map/reduce_scatter | solution.py:197
  551.3 3.7 fusion.116
  554.9 88.9 %reduce-scatter.11.cloned.1.call-done = bf16[128,2,1024]{2,0,1:T(8,128)(2,1)} async-done(((bf16[1024,2,1024]{2,0,1:T(8,128)(2,1)}), bf16[128,2,1024]{2,0,1:T(8,128)(2,1)}) %reduce-scatter.11.cloned.1.call-update) | async-done | bytes 524304 | tf_op jit(solution)/shard_map/reduce_scatter | solution.py:197
  643.8 4.3 fusion.58
  653.4 8.2 fusion.169
  661.6 11.9 %add_convert_fusion.1 = bf16[1024,4096]{1,0:T(8,128)(2,1)} fusion(f32[1024,4096]{1,0:T(8,128)} %fusion.169, bf16[128,4096]{1,0:T(8,128)(2,1)S(1)} %copy-done.37, f32[128,1024]{1,0:T(8,128)S(1)} %copy-done.20, f32[128]{0:T(128)S(1)} %add_rsqrt_fusion.1, f32[128]{0:T(128)S(1)} %broadcast_multiply_fusion.9, f32[1024]{0:T(1024)S(1)} %bitcast.391, ...), kind=kOutput, calls=%fused_computation.51 | convolution fusion | flops 1082785792 | bytes 26747904 | tf_op jit(solution)/shard_map/dot_general | solution.py:40
  675.1 10.9 fusion.153
  686.0 12.7 %add_convert_fusion = bf16[4096,1024]{1,0:T(8,128)(2,1)} fusion(f32[4096,1024]{1,0:T(8,128)} %fusion.153, f32[128,1024]{1,0:T(8,128)S(1)} %copy-done.52, f32[128,4096]{1,0:T(8,128)S(1)} %copy-done.47), kind=kOutput, calls=%fused_computation.50 | convolution fusion | flops 1116340224 | bytes 27787264 | tf_op jit(solution)/shard_map/dot_general | solution.py:40
  699.1 12.4 %reduce-scatter.19.cloned.1.call-done = bf16[256,1024]{1,0:T(8,128)(2,1)} async-done(((bf16[1024,1024]{1,0:T(8,128)(2,1)}), bf16[256,1024]{1,0:T(8,128)(2,1)}) %reduce-scatter.19.cloned.1.call-update) | async-done | bytes 524304 | tf_op jit(solution)/shard_map/reduce_scatter | solution.py:410
  711.5 34.4 %reduce-scatter.15.cloned.1.call-done = bf16[256,1024]{0,1:T(8,128)(2,1)} async-done(((bf16[1024,1024]{0,1:T(8,128)(2,1)}), bf16[256,1024]{0,1:T(8,128)(2,1)}) %reduce-scatter.15.cloned.1.call-update) | async-done | bytes 524304 | tf_op jit(solution)/shard_map/reduce_scatter | solution.py:410
  745.9 34.5 %reduce-scatter.17.cloned.1.call-done = bf16[256,1024]{0,1:T(8,128)(2,1)} async-done(((bf16[1024,1024]{0,1:T(8,128)(2,1)}), bf16[256,1024]{0,1:T(8,128)(2,1)}) %reduce-scatter.17.cloned.1.call-update) | async-done | bytes 524304 | tf_op jit(solution)/shard_map/reduce_scatter | solution.py:410
  780.5 74.2 %reduce-scatter.21.cloned.1.call-done = bf16[256,4096]{1,0:T(8,128)(2,1)} async-done(((bf16[1024,4096]{1,0:T(8,128)(2,1)}), bf16[256,4096]{1,0:T(8,128)(2,1)}) %reduce-scatter.21.cloned.1.call-update) | async-done | bytes 2097168 | tf_op jit(solution)/shard_map/reduce_scatter | solution.py:410
  854.7 74.4 %reduce-scatter.23.cloned.1.call-done = bf16[1024,1024]{1,0:T(8,128)(2,1)} async-done(((bf16[4096,1024]{1,0:T(8,128)(2,1)}), bf16[1024,1024]{1,0:T(8,128)(2,1)}) %reduce-scatter.23.cloned.1.call-update) | async-done | bytes 2097168 | tf_op jit(solution)/shard_map/reduce_scatter | solution.py:410
  934.8 2.6 convolution_add_fusion.4
  939.2 11.3 all-reduce.11
  951.1 23.2 %all-reduce.9 = (bf16[256]{0:T(256)(128)(2,1)S(1)}, bf16[256]{0:T(256)(128)(2,1)S(1)}, bf16[256]{0:T(256)(128)(2,1)S(1)}, bf16[256]{0:T(256)(128)(2,1)S(1)}, bf1...) all-reduce(bf16[256]{0:T(256)(128)(2,1)S(1)} %dynamic-slice.1, ...), channel_id=1, replica_groups=mesh['ctx'=8,'fsdp'=4] {'ctx'}, use_global_device_ids=true, to_apply=%region_43.45 | all-reduce | flops 3072 | bytes 12288 | tf_op jit(solution)/shard_map/psum | solution.py:412
  979.4 2.6 convolution_add_fusion.3
  986.5 164.3 %all-reduce.14.cloned.1.call-done = (bf16[256,1024]{0,1:T(8,128)(2,1)}, bf16[256,1024]{0,1:T(8,128)(2,1)}, bf16[256,1024]{0,1:T(8,128)(2,1)}, bf16[256,1024]{1,0...) async-done(((bf16[256,1024]{0,1:T(8,128)(2,1)}, bf16[256,1024]{0,1:T(8,128)(2,1)}, bf16[256,1024]{0,1:T(8,128)(2,1)}, bf16[256,1024]{1,0:T(8,128)(2,1)}, ...) | async-done | bytes 6291472 | tf_op jit(solution)/shard_map/psum | solution.py:412
  1157.7 2.5 convert_element_type.463
  (432 shorter events, 123.8 us)
Async XLA Ops:
  7.2 27.7 %all-gather.26.cloned.1.call-start = ((), (), s32[]{:S(2)}) async-start(), calls=%async_computation.11 | async-start | bytes 2621440 | tf_op jit(solution)/shard_map/all_gather | solution.py:72
  7.9 51.2 %copy-start.13 = (bf16[2,1,128,1024]{3,2,1,0:T(8,128)(2,1)S(1)}, bf16[2,1,128,1024]{3,2,1,0:T(8,128)(2,1)}, u32[]{:S(2)}) copy-start(bf16[2,1,128,1024]{3,2,1,0:T(8,128)(2,1)} %param.24) | copy-start | bytes 1572868
  7.9 51.2 %all-gather.22.cloned.1.call-start = ((), (), s32[]{:S(2)}) async-start(), calls=%async_computation.9 | async-start | bytes 2621440 | tf_op jit(solution)/shard_map/all_gather | solution.py:71
  8.7 265.1 %all-gather.20.cloned.1.call-start = ((), (), s32[]{:S(2)}) async-start(), calls=%async_computation.8 | async-start | bytes 2621440 | tf_op jit(solution)/shard_map/all_gather | solution.py:70
  9.4 284.4 %all-gather.28.cloned.1.call-start = ((), (), s32[]{:S(2)}) async-start(), calls=%async_computation.12 | async-start | bytes 2359296 | tf_op jit(solution)/shard_map/all_gather | solution.py:94
  37.7 24.2 %copy-start.6 = (bf16[1024,1024]{1,0:T(8,128)(2,1)S(1)}, bf16[1024,1024]{1,0:T(8,128)(2,1)}, u32[]{:S(2)}) copy-start(bf16[1024,1024]{1,0:T(8,128)(2,1)} %all-gather.26.cloned.1.call-done) | copy-start | bytes 6291460
  37.8 260.0 %all-gather.24.cloned.1.call-start = ((), (), s32[]{:S(2)}) async-start(), calls=%async_computation.10 | async-start | bytes 2359296 | tf_op jit(solution)/shard_map/all_gather | solution.py:93
  61.9 249.9 %all-gather.36.cloned.1.call-start = ((), (), s32[]{:S(2)}) async-start(), calls=%async_computation.16 | async-start | bytes 2359296 | tf_op jit(solution)/shard_map/all_gather | solution.py:94
  63.1 252.7 %all-gather.34.cloned.1.call-start = ((), (), s32[]{:S(2)}) async-start(), calls=%async_computation.15 | async-start | bytes 2359296 | tf_op jit(solution)/shard_map/all_gather | solution.py:93
  66.0 253.7 %all-gather.30.cloned.1.call-start = ((), (), s32[]{:S(2)}) async-start(), calls=%async_computation.13 | async-start | bytes 2621440 | tf_op jit(solution)/shard_map/all_gather | solution.py:73
  66.8 307.8 %all-gather.32.cloned.1.call-start = ((), (), s32[]{:S(2)}) async-start(), calls=%async_computation.14 | async-start | bytes 10485760 | tf_op jit(solution)/shard_map/all_gather | solution.py:74
  66.9 35.0 %collective-permute-start = (bf16[1024,1024]{1,0:T(8,128)(2,1)S(1)}, bf16[1024,1024]{1,0:T(8,128)(2,1)}, u32[]{:S(2)}, u32[]{:S(2)}) collective-permute-start(bf16[1024,1024]{1,0:T(8,128)(2,1)S(1)} %copy-done.27), channel_id=1, source_target_pairs={{0,3},{1,0},{2,1},{3,2},{4,7},{5,4},{6,5},{7,6},{8,11},{9,8},{10,9... | collective-permute-start | bytes 6291464 | tf_op jit(solution)/shard_map/ppermute | solution.py:22
  67.5 40.1 %copy-start.92 = (bf16[256]{0:T(256)(128)(2,1)S(1)}, bf16[256]{0:T(256)(128)(2,1)}, u32[]{:S(2)}) copy-start(bf16[256]{0:T(256)(128)(2,1)} %param.39) | copy-start | bytes 1540
  67.5 132.6 %copy-start.90 = (bf16[1024]{0:T(1024)(128)(2,1)S(1)}, bf16[1024]{0:T(1024)(128)(2,1)}, u32[]{:S(2)}) copy-start(bf16[1024]{0:T(1024)(128)(2,1)} %param.38) | copy-start | bytes 6148
  67.6 138.1 %copy-start.93 = (bf16[256]{0:T(256)(128)(2,1)S(1)}, bf16[256]{0:T(256)(128)(2,1)}, u32[]{:S(2)}) copy-start(bf16[256]{0:T(256)(128)(2,1)} %param.35) | copy-start | bytes 1540
  67.6 143.1 %copy-start.91 = (s32[2,1,128]{2,1,0:T(1,128)S(1)}, s32[2,1,128]{2,1,0:T(1,128)}, u32[]{:S(2)}) copy-start(s32[2,1,128]{2,1,0:T(1,128)} %param.25) | copy-start | bytes 3076
  67.6 143.1 %copy-start.94 = (bf16[256]{0:T(256)(128)(2,1)S(1)}, bf16[256]{0:T(256)(128)(2,1)}, u32[]{:S(2)}) copy-start(bf16[256]{0:T(256)(128)(2,1)} %param.33) | copy-start | bytes 1540
  67.6 148.2 %copy-start.95 = (bf16[256]{0:T(256)(128)(2,1)S(1)}, bf16[256]{0:T(256)(128)(2,1)}, u32[]{:S(2)}) copy-start(bf16[256]{0:T(256)(128)(2,1)} %param.37) | copy-start | bytes 1540
  67.6 153.3 %copy-start.96 = (bf16[256]{0:T(256)(128)(2,1)S(1)}, bf16[256]{0:T(256)(128)(2,1)}, u32[]{:S(2)}) copy-start(bf16[256]{0:T(256)(128)(2,1)} %param.36) | copy-start | bytes 1540
  67.6 158.4 %copy-start.97 = (bf16[256]{0:T(256)(128)(2,1)S(1)}, bf16[256]{0:T(256)(128)(2,1)}, u32[]{:S(2)}) copy-start(bf16[256]{0:T(256)(128)(2,1)} %param.40) | copy-start | bytes 1540
  67.6 200.1 %copy-start.98 = (bf16[256]{0:T(256)(128)(2,1)S(1)}, bf16[256]{0:T(256)(128)(2,1)}, u32[]{:S(2)}) copy-start(bf16[256]{0:T(256)(128)(2,1)} %param.41) | copy-start | bytes 1540
  67.6 483.6 %reduce-scatter.9.cloned.1.call-start = ((), (), s32[]{:S(2)}) async-start(), calls=%async_computation.17 | async-start | bytes 4718592 | tf_op jit(solution)/shard_map/reduce_scatter | solution.py:197
  105.9 170.9 %collective-permute-start.1 = (bf16[2048,1024]{1,0:T(8,128)(2,1)}, bf16[2048,1024]{1,0:T(8,128)(2,1)}, u32[]{:S(2)}, u32[]{:S(2)}) collective-permute-start(bf16[2048,1024]{1,0:T(8,128)(2,1)} %pad_maximum_fusion), channel_id=1, source_target_pairs={{0,2},{1,3},{2,0},{3,1},{4,6},{5,7},{6,4},{7,5},{8,10},{9,11},{10,... | collective-permute-start | bytes 12582920 | tf_op jit(solution)/shard_map/ppermute | solution.py:22
  220.9 169.8 %copy-start.57 = (f32[4,1,256]{2,1,0:T(1,128)}, f32[4,1,256]{2,1,0:T(1,128)S(1)}, u32[]{:S(2)}) copy-start(f32[4,1,256]{2,1,0:T(1,128)S(1)} %convert_element_type.499) | copy-start | bytes 12292
  231.1 45.5 %copy-start.71 = (bf16[128]{0:T(256)(128)(2,1)}, bf16[128]{0:T(256)(128)(2,1)S(1)}, u32[]{:S(2)}) copy-start(bf16[128]{0:T(256)(128)(2,1)S(1)} %get-tuple-element.655) | copy-start | bytes 772
  231.1 45.5 %copy-start.73 = (bf16[128]{0:T(256)(128)(2,1)}, bf16[128]{0:T(256)(128)(2,1)S(1)}, u32[]{:S(2)}) copy-start(bf16[128]{0:T(256)(128)(2,1)S(1)} %get-tuple-element.703) | copy-start | bytes 772
  251.5 25.1 %copy-start.67 = (bf16[1024]{0:T(1024)(128)(2,1)}, bf16[1024]{0:T(1024)(128)(2,1)S(1)}, u32[]{:S(2)}) copy-start(bf16[1024]{0:T(1024)(128)(2,1)S(1)} %reduce.4) | copy-start | bytes 6148
  267.7 8.9 copy-start.65
  276.8 45.3 %copy-start.4 = (bf16[128,1024]{0,1:T(8,128)(2,1)}, bf16[128,1024]{0,1:T(8,128)(2,1)S(1)}, u32[]{:S(2)}) copy-start(bf16[128,1024]{0,1:T(8,128)(2,1)S(1)} %copy.100) | copy-start | bytes 786436
  310.8 8.9 copy-start.32
  321.9 97.4 %copy-start.15 = (f32[128,1024]{1,0:T(8,128)}, f32[128,1024]{1,0:T(8,128)S(1)}, u32[]{:S(2)}) copy-start(f32[128,1024]{1,0:T(8,128)S(1)} %get-tuple-element.471) | copy-start | bytes 1572868
  321.9 97.3 %copy-start.75 = (f32[128]{0:T(128)}, f32[128]{0:T(128)S(1)}, u32[]{:S(2)}) copy-start(f32[128]{0:T(128)S(1)} %broadcast_multiply_fusion.11) | copy-start | bytes 1540
  333.5 85.8 %copy-start.77 = (f32[128]{0:T(128)}, f32[128]{0:T(128)S(1)}, u32[]{:S(2)}) copy-start(f32[128]{0:T(128)S(1)} %add_rsqrt_fusion.3) | copy-start | bytes 1540
  374.6 16.1 %slice-start.2 = ((s8[8388608]{0:T(1024)(128)(4,1)}), s8[4194304]{0:T(1024)(128)(4,1)S(1)}, s32[]{:S(2)}) async-start(s8[8388608]{0:T(1024)(128)(4,1)} %bitcast.365), calls=%async_computation.28 | async-start | bytes 8388608
  379.5 19.9 %copy-start.44 = (f32[128,4096]{1,0:T(8,128)}, f32[128,4096]{1,0:T(8,128)S(1)}, u32[]{:S(2)}) copy-start(f32[128,4096]{1,0:T(8,128)S(1)} %convolution_add_fusion.1) | copy-start | bytes 6291460
  379.5 9.8 slice-start
  379.5 9.8 slice-start.1
  379.5 9.8 copy-start.18
  379.5 11.1 slice-start.3
  390.7 20.5 %copy-start.46 = (f32[128,4096]{1,0:T(8,128)}, f32[128,4096]{1,0:T(8,128)S(1)}, u32[]{:S(2)}) copy-start(f32[128,4096]{1,0:T(8,128)S(1)} %convolution_add_fusion) | copy-start | bytes 6291460
  390.7 5.8 copy-start.31
  399.4 8.1 copy-start.53
  399.4 19.9 %copy-start.51 = (f32[128,1024]{1,0:T(8,128)}, f32[128,1024]{1,0:T(8,128)S(1)}, u32[]{:S(2)}) copy-start(f32[128,1024]{1,0:T(8,128)S(1)} %get-tuple-element.440) | copy-start | bytes 1572868
  463.1 180.7 %reduce-scatter.11.cloned.1.call-start = ((), (), s32[]{:S(2)}) async-start(), calls=%async_computation.18 | async-start | bytes 4718592 | tf_op jit(solution)/shard_map/reduce_scatter | solution.py:197
  506.9 192.2 %reduce-scatter.13.cloned.1.call-start = ((), (), s32[]{:S(2)}) async-start(), calls=%async_computation.19 | async-start | bytes 2621440 | tf_op jit(solution)/shard_map/reduce_scatter | solution.py:410
  511.2 200.3 %reduce-scatter.19.cloned.1.call-start = ((), (), s32[]{:S(2)}) async-start(), calls=%async_computation.22 | async-start | bytes 2621440 | tf_op jit(solution)/shard_map/reduce_scatter | solution.py:410
  515.1 230.8 %reduce-scatter.15.cloned.1.call-start = ((), (), s32[]{:S(2)}) async-start(), calls=%async_computation.20 | async-start | bytes 2621440 | tf_op jit(solution)/shard_map/reduce_scatter | solution.py:410
  648.2 132.3 %reduce-scatter.17.cloned.1.call-start = ((), (), s32[]{:S(2)}) async-start(), calls=%async_computation.21 | async-start | bytes 2621440 | tf_op jit(solution)/shard_map/reduce_scatter | solution.py:410
  652.0 9.6 copy-start.20
  652.0 202.6 %reduce-scatter.21.cloned.1.call-start = ((), (), s32[]{:S(2)}) async-start(), calls=%async_computation.23 | async-start | bytes 10485760 | tf_op jit(solution)/shard_map/reduce_scatter | solution.py:410
  653.4 8.2 copy-start.37
  673.5 255.5 %reduce-scatter.23.cloned.1.call-start = ((), (), s32[]{:S(2)}) async-start(), calls=%async_computation.24 | async-start | bytes 10485760 | tf_op jit(solution)/shard_map/reduce_scatter | solution.py:410
  675.1 10.9 copy-start.47
  675.1 10.9 copy-start.52
  698.8 452.0 %all-reduce.14.cloned.1.call-start = ((), (), s32[]{:S(2)}) async-start(), calls=%async_computation.25 | async-start | bytes 12582912 | tf_op jit(solution)/shard_map/psum | solution.py:412
  929.1 5.7 copy-start.83
  929.1 5.7 copy-start.81
  929.1 5.7 copy-start.82
  929.1 5.7 copy-start.88
  929.1 5.7 copy-start.89
  929.1 5.7 copy-start.10
  939.0 42.9 %copy-start.7 = (bf16[1024,1024]{1,0:T(8,128)(2,1)S(1)}, bf16[1024,1024]{1,0:T(8,128)(2,1)}, u32[]{:S(2)}) copy-start(bf16[1024,1024]{1,0:T(8,128)(2,1)} %all-gather.26.cloned.1.call-done) | copy-start | bytes 6291460
  939.0 42.9 %copy-start.42 = (bf16[128,2,1024]{2,0,1:T(8,128)(2,1)S(1)}, bf16[128,2,1024]{2,0,1:T(8,128)(2,1)}, u32[]{:S(2)}) copy-start(bf16[128,2,1024]{2,0,1:T(8,128)(2,1)} %reduce-scatter.11.cloned.1.call-done) | copy-start | bytes 1572868
  1150.7 5.9 copy-start.59
  (66 other events, 159.0 us)
Sparse Core Ops, SparseCore 0:
  9.6 25.2 all-gather.25
  36.5 22.5 all-gather.21
  60.7 28.2 all-gather.19
  91.5 49.2 all-gather.27
  143.3 47.7 all-gather.23
  193.7 47.7 all-gather.35
  244.2 47.8 all-gather.33
  293.7 20.9 all-gather.29
  316.3 58.2 all-gather.31
  463.2 88.0 reduce-scatter.8
  555.9 87.8 reduce-scatter.10
  646.2 31.1 reduce-scatter.12
  680.1 31.3 reduce-scatter.18
  714.5 31.4 reduce-scatter.14
  749.0 31.3 reduce-scatter.16
  782.9 71.7 reduce-scatter.20
  857.3 71.7 reduce-scatter.22
  933.9 216.7 all-reduce.13
